TPU v7x, 512 devices: a whole 4x4x16 slice. The times are simulated.
512 devices in a mesh: slab: 64 (over z, x_hi, core), band: 8 (over y, x_lo).
Axes of the slice: x: 4 (x_hi: 2, x_lo: 2; x = x_hi * 2 + x_lo), y: 4, z: 16, core: 2. Of those that a mesh axis runs over, the one named last changes fastest.
Arguments:
- hamiltonian: bfloat16 [512, 7, 128, 128], P('slab', None, 'band'), may hold values from -0.1875 to 0.1875
- neighbors: int32 [512, 7], P('slab'), may hold values from 0 to 11, as said below
- orbitals: bfloat16 [65536, 1024], P('slab', 'band'), may hold values from -6 to 6
Outputs:
- residual: bfloat16 [65536, 1024], P(('slab', 'band'))
Inputs may be any that keep to these rules, and one draw needn't show every extreme that they name: `neighbors`: window positions 0 to 1 are the last 2 elements of the slab below (periodic), 2 to 9 the slab's own elements, the rest the first 2 elements of the slab above. A slab's elements are in layers of 2; each block row names, in an order of its own, itself, the element 2 positions below and above it in the window, and four elements of its own layer (repeats possible).
All inputs are finite; a program needn't handle non-finite values.
Results may differ from a plain program's by a relative error of at most 0.012.
Values may be sent and summed in bfloat16 or wider, within the bound.
No kernel may reach another device: no remote copies, remote signals or barrier semaphores. Data moves between devices by JAX's collectives and lax.ppermute only.
A program may use at most 64 MiB of HBM per device.

v0:
```python
import math
import jax
import jax.numpy as jnp
from jax import lax
from jax.sharding import PartitionSpec as P

FACE = 2


def padded(block, sides, width):
    for axis, dim in sides:
        count = lax.axis_size(axis)
        forward = [(i, i + 1) for i in range(count - 1)]
        forward.append((count - 1, 0))
        backward = [(target, source) for source, target in forward]
        low = lax.ppermute(
            lax.slice_in_dim(block, block.shape[dim] - width, None, axis=dim), axis, forward
        )
        high = lax.ppermute(lax.slice_in_dim(block, 0, width, axis=dim), axis, backward)
        block = jnp.concatenate([low, block, high], axis=dim)
    return block


def apply_local(vector, full_tiles, neighbors):
    tile_size = full_tiles.shape[2]
    extended = padded(vector, (("slab", 0),), FACE * tile_size)
    blocks = extended.reshape(-1, tile_size, vector.shape[1])
    picked_blocks = blocks[neighbors]
    product = jnp.einsum(
        "rjab,rjbc->rac", full_tiles, picked_blocks, preferred_element_type=jnp.float32
    )
    return product.reshape(vector.shape[0], vector.shape[1])


def body(hamiltonian, neighbors, orbitals):
    full_tiles = lax.all_gather(hamiltonian, "band", axis=2, tiled=True)
    first = apply_local(orbitals, full_tiles, neighbors).astype(jnp.bfloat16)
    second = (
        2.0 * apply_local(first, full_tiles, neighbors) - orbitals.astype(jnp.float32)
    ).astype(jnp.bfloat16)
    third = (2.0 * apply_local(second, full_tiles, neighbors) - first.astype(jnp.float32)).astype(
        jnp.bfloat16
    )
    applied = apply_local(third, full_tiles, neighbors).astype(jnp.bfloat16)
    rows_all = orbitals.shape[0] * lax.axis_size("slab")
    bands_all = orbitals.shape[1] * lax.axis_size("band")
    gram_scale = 1.0 / math.sqrt(float(rows_all) * float(bands_all))
    strip_third, strip_applied = (
        lax.all_to_all(third, "band", split_axis=0, concat_axis=1, tiled=True),
        lax.all_to_all(applied, "band", split_axis=0, concat_axis=1, tiled=True),
    )
    partial_value = jnp.einsum(
        "rb,rc->bc", strip_third, strip_applied, preferred_element_type=jnp.float32
    )
    summed = lax.psum(partial_value, ("slab", "band"))
    gram_full = (summed * gram_scale).astype(jnp.bfloat16)
    mixed = jnp.dot(strip_third, gram_full, preferred_element_type=jnp.float32)
    return (strip_applied.astype(jnp.float32) - mixed).astype(jnp.bfloat16)


def solution(mesh):
    in_specs = (P("slab", None, "band", None), P("slab", None), P("slab", "band"))
    out_specs = P(("slab", "band"), None)
    return jax.shard_map(body, mesh=mesh, in_specs=in_specs, out_specs=out_specs, check_vma=False)
```

profile of v0, /device:TPU:2, one launch (start us, length us, event | category | flops | bytes accessed | tf_op | source)
XLA Modules:
  0.0 640.3 jit_solution(16940214057220224389)
XLA Ops:
  6.5 0.7 all-gather.2.cloned.1.call-update
  7.3 0.9 fusion.16
  8.1 1.9 collective-permute-start
  10.1 12.4 %collective-permute-start.1 = (bf16[256,128]{1,0:T(8,128)(2,1)S(1)}, bf16[256,128]{1,0:T(8,128)(2,1)S(1)}, u32[]{:S(2)}, u32[]{:S(2)}) collective-permute-start(bf16[256,128]{1,0:T(8,128)(2,1)S(1)} %get-tuple-element.12), channel_id=1, source_target_pairs={{8,0},{16,8},{24,16},{32,24},{40,32},{48,40},{56,48},{64,56},{72,6... | collective-permute-start | bytes 196616 | tf_op jit(solution)/shard_map/ppermute | solution.py:19
  22.5 0.7 compare_select_fusion
  23.3 1.1 collective-permute-done.1
  24.4 1.0 pad_maximum_fusion
  25.3 0.9 gather_fusion
  26.3 42.6 %all-gather.2.cloned.1.call-done = bf16[8,7,128,128]{3,2,1,0:T(8,128)(2,1)} async-done(((bf16[8,7,16,128]{3,2,1,0:T(8,128)(2,1)}), bf16[8,7,128,128]{3,2,1,0:T(8,128)(2,1)}) %all-gather.2.cloned.1.call-update) | async-done | bytes 1835024 | tf_op jit(solution)/shard_map/all_gather | solution.py:36
  68.9 2.1 fusion.6
  71.0 3.2 collective-permute-start.3
  74.2 1.9 collective-permute-start.2
  76.2 7.3 %collective-permute-done.2 = bf16[256,128]{1,0:T(8,128)(2,1)S(1)} collective-permute-done((bf16[256,128]{1,0:T(8,128)(2,1)S(1)}, bf16[256,128]{1,0:T(8,128)(2,1)S(1)}, u32[]{:S(2)}, u32[]{:S(2)}) %collective-permute-start.2) | collective-permute-done | bytes 65568 | tf_op jit(solution)/shard_map/ppermute | solution.py:16
  83.5 2.0 gather_fusion.1
  85.5 2.2 fusion.3
  87.8 1.9 collective-permute-start.4
  89.7 7.3 %collective-permute-start.5 = (bf16[256,128]{1,0:T(8,128)(2,1)S(1)}, bf16[256,128]{1,0:T(8,128)(2,1)S(1)}, u32[]{:S(2)}, u32[]{:S(2)}) collective-permute-start(bf16[256,128]{1,0:T(8,128)(2,1)S(1)} %get-tuple-element.8), channel_id=1, source_target_pairs={{8,0},{16,8},{24,16},{32,24},{40,32},{48,40},{56,48},{64,56},{72,6... | collective-permute-start | bytes 196616 | tf_op jit(solution)/shard_map/ppermute | solution.py:19
  97.0 1.9 collective-permute-done.5
  98.9 2.1 gather_fusion.2
  101.0 2.1 fusion.4
  103.2 1.9 collective-permute-start.6
  105.1 7.3 %collective-permute-start.7 = (bf16[256,128]{1,0:T(8,128)(2,1)S(1)}, bf16[256,128]{1,0:T(8,128)(2,1)S(1)}, u32[]{:S(2)}, u32[]{:S(2)}) collective-permute-start(bf16[256,128]{1,0:T(8,128)(2,1)S(1)} %get-tuple-element.6), channel_id=1, source_target_pairs={{8,0},{16,8},{24,16},{32,24},{40,32},{48,40},{56,48},{64,56},{72,6... | collective-permute-start | bytes 196616 | tf_op jit(solution)/shard_map/ppermute | solution.py:19
  112.4 0.8 fusion.11
  113.2 6.0 all-to-all-start.1
  119.3 2.1 gather_fusion.3
  121.4 3.0 fusion.8
  124.3 1.0 all-to-all-done.1
  125.4 4.7 all-to-all-start
  130.2 5.9 all-to-all-done
  136.2 2.7 fusion.17
  139.0 491.1 %all-reduce.2.cloned.1.call-done = f32[1024,1024]{1,0:T(8,128)} async-done(((f32[1024,1024]{1,0:T(8,128)}), f32[1024,1024]{1,0:T(8,128)}) %all-reduce.2.cloned.1.call-update) | async-done | bytes 4194320 | tf_op jit(solution)/shard_map/psum | solution.py:55
  630.1 3.4 fusion.7
  (24 shorter events, 0.7 us)
Async XLA Ops:
  6.5 62.3 %all-gather.2.cloned.1.call-start = ((), (), s32[]{:S(2)}) async-start(), calls=%async_computation.2 | async-start | bytes 2064384 | tf_op jit(solution)/shard_map/all_gather | solution.py:36
  8.1 15.1 %collective-permute-start = (bf16[256,128]{1,0:T(8,128)(2,1)S(1)}, bf16[256,128]{1,0:T(8,128)(2,1)S(1)}, u32[]{:S(2)}, u32[]{:S(2)}) collective-permute-start(bf16[256,128]{1,0:T(8,128)(2,1)S(1)} %get-tuple-element.11), channel_id=1, source_target_pairs={{0,8},{8,16},{16,24},{24,32},{32,40},{40,48},{48,56},{56,64},{64,7... | collective-permute-start | bytes 196616 | tf_op jit(solution)/shard_map/ppermute | solution.py:16
  10.1 14.3 %collective-permute-start.1 = (bf16[256,128]{1,0:T(8,128)(2,1)S(1)}, bf16[256,128]{1,0:T(8,128)(2,1)S(1)}, u32[]{:S(2)}, u32[]{:S(2)}) collective-permute-start(bf16[256,128]{1,0:T(8,128)(2,1)S(1)} %get-tuple-element.12), channel_id=1, source_target_pairs={{8,0},{16,8},{24,16},{32,24},{40,32},{48,40},{56,48},{64,56},{72,6... | collective-permute-start | bytes 196616 | tf_op jit(solution)/shard_map/ppermute | solution.py:19
  71.0 5.2 collective-permute-start.3
  74.2 9.2 %collective-permute-start.2 = (bf16[256,128]{1,0:T(8,128)(2,1)S(1)}, bf16[256,128]{1,0:T(8,128)(2,1)S(1)}, u32[]{:S(2)}, u32[]{:S(2)}) collective-permute-start(bf16[256,128]{1,0:T(8,128)(2,1)S(1)} %bitcast.83), channel_id=1, source_target_pairs={{0,8},{8,16},{16,24},{24,32},{32,40},{40,48},{48,56},{56,64},{64,7... | collective-permute-start | bytes 196616 | tf_op jit(solution)/shard_map/ppermute | solution.py:16
  83.5 2.0 copy-start
  85.5 2.2 copy-start.1
  87.8 9.2 %collective-permute-start.4 = (bf16[256,128]{1,0:T(8,128)(2,1)S(1)}, bf16[256,128]{1,0:T(8,128)(2,1)S(1)}, u32[]{:S(2)}, u32[]{:S(2)}) collective-permute-start(bf16[256,128]{1,0:T(8,128)(2,1)S(1)} %get-tuple-element.7), channel_id=1, source_target_pairs={{0,8},{8,16},{16,24},{24,32},{32,40},{40,48},{48,56},{56,64},{64,7... | collective-permute-start | bytes 196616 | tf_op jit(solution)/shard_map/ppermute | solution.py:16
  89.7 9.1 %collective-permute-start.5 = (bf16[256,128]{1,0:T(8,128)(2,1)S(1)}, bf16[256,128]{1,0:T(8,128)(2,1)S(1)}, u32[]{:S(2)}, u32[]{:S(2)}) collective-permute-start(bf16[256,128]{1,0:T(8,128)(2,1)S(1)} %get-tuple-element.8), channel_id=1, source_target_pairs={{8,0},{16,8},{24,16},{32,24},{40,32},{48,40},{56,48},{64,56},{72,6... | collective-permute-start | bytes 196616 | tf_op jit(solution)/shard_map/ppermute | solution.py:19
  103.2 16.1 %collective-permute-start.6 = (bf16[256,128]{1,0:T(8,128)(2,1)S(1)}, bf16[256,128]{1,0:T(8,128)(2,1)S(1)}, u32[]{:S(2)}, u32[]{:S(2)}) collective-permute-start(bf16[256,128]{1,0:T(8,128)(2,1)S(1)} %get-tuple-element.5), channel_id=1, source_target_pairs={{0,8},{8,16},{16,24},{24,32},{32,40},{40,48},{48,56},{56,64},{64,7... | collective-permute-start | bytes 196616 | tf_op jit(solution)/shard_map/ppermute | solution.py:16
  105.1 14.1 %collective-permute-start.7 = (bf16[256,128]{1,0:T(8,128)(2,1)S(1)}, bf16[256,128]{1,0:T(8,128)(2,1)S(1)}, u32[]{:S(2)}, u32[]{:S(2)}) collective-permute-start(bf16[256,128]{1,0:T(8,128)(2,1)S(1)} %get-tuple-element.6), channel_id=1, source_target_pairs={{8,0},{16,8},{24,16},{32,24},{40,32},{48,40},{56,48},{64,56},{72,6... | collective-permute-start | bytes 196616 | tf_op jit(solution)/shard_map/ppermute | solution.py:19
  113.2 12.2 %all-to-all-start.1 = ((bf16[8,128,128]{2,1,0:T(8,128)(2,1)}), bf16[8,128,128]{2,1,0:T(8,128)(2,1)S(1)}, u32[]{:S(2)}, u32[]{:S(2)}) async-start(bf16[8,128,128]{2,1,0:T(8,128)(2,1)} %fusion.11), calls=%async_computation.1 | async-start | bytes 524288 | tf_op jit(solution)/shard_map/all_to_all | solution.py:49
  125.4 10.8 %all-to-all-start = ((bf16[8,128,128]{1,2,0:T(8,128)(2,1)}), bf16[8,128,128]{1,2,0:T(8,128)(2,1)S(1)}, u32[]{:S(2)}, u32[]{:S(2)}) async-start(bf16[8,128,128]{1,2,0:T(8,128)(2,1)} %fusion.8), calls=%async_computation | async-start | bytes 524288 | tf_op jit(solution)/shard_map/all_to_all | solution.py:50
  130.0 500.1 %all-reduce.2.cloned.1.call-start = ((), (), s32[]{:S(2)}) async-start(), calls=%async_computation.3 | async-start | bytes 8388608 | tf_op jit(solution)/shard_map/psum | solution.py:55
Sparse Core Ops, SparseCore 0:
  9.3 59.4 all-gather.1
  139.0 491.0 all-reduce.1
where the time goes:
time: 641 us; the launch traced here: 640 us
  waiting for transfers between devices  552 us (86%)
  starting transfers between devices  48.6 us (8%)
  matrix products  15.5 us (2%)
  between operations  13.6 us (2%)
  local copies, waits for them, and re-layouts  8.39 us (1%)
    psum x1, waiting for transfers between devices, body(): summed = lax.psum(partial_value, ('slab', 'band'))  491 us
    all_gather x1, waiting for transfers between devices, body(): full_tiles = lax.all_gather(hamiltonian, 'band', axis=2, tiled=True)  42.6 us
    ppermute x4, starting transfers between devices, padded(): lax.ppermute(lax.slice_in_dim(block, 0, width, axis=dim), axis, backward)  30.2 us
  transfers between devices with their start and end apart: 12, of which 7 were waited for; matrix products, arithmetic and copies ran while one was open for 2% of the time, Pallas kernels for 0%

commit v1 on v0

--- a/solution.py
+++ b/solution.py
@@ -33,7 +33,9 @@
 
 
 def body(hamiltonian, neighbors, orbitals):
-    full_tiles = lax.all_gather(hamiltonian, "band", axis=2, tiled=True)
+    full_tiles = jnp.concatenate(
+        lax.all_to_all(jnp.stack([hamiltonian] * lax.axis_size("band")), "band", 0, 0), axis=2
+    )
     first = apply_local(orbitals, full_tiles, neighbors).astype(jnp.bfloat16)
     second = (
         2.0 * apply_local(first, full_tiles, neighbors) - orbitals.astype(jnp.float32)

time: 641 us -> 615 us (0.959)
  waiting for transfers between devices: 552 us -> 510 us
  starting transfers between devices: 48.6 us -> 61.9 us
    all_gather x1 -> x0, waiting for transfers between devices: 42.6 us -> none  [body(): full_tiles = lax.all_gather(hamiltonian, 'band', axis=2, tiled=True)]
    all_to_all x0 -> x1, starting transfers between devices: none -> 10.2 us  [body(): lax.all_to_all(jnp.stack([hamiltonian] * lax.axis_size('band')), 'band',...]
  transfers between devices with their start and end apart: 12 -> 12, of which waited for: 7 -> 7; matrix products, arithmetic and copies ran while one was open for 2% -> 1% of each run, Pallas kernels for 0% -> 0%
where the time goes in v1:
time: 615 us; the launch traced here: 614 us
  waiting for transfers between devices  510 us (83%)
  starting transfers between devices  61.9 us (10%)
  matrix products  13.9 us (2%)
  between operations  13.6 us (2%)
  local copies, waits for them, and re-layouts  13.3 us (2%)
    psum x1, waiting for transfers between devices, body(): summed = lax.psum(partial_value, ('slab', 'band'))  487 us
    ppermute x4, starting transfers between devices, padded(): lax.ppermute(lax.slice_in_dim(block, 0, width, axis=dim), axis, backward)  33.5 us
  transfers between devices with their start and end apart: 12, of which 7 were waited for; matrix products, arithmetic and copies ran while one was open for 1% of the time, Pallas kernels for 0%

profile of v1, /device:TPU:2, one launch (start us, length us, event | category | flops | bytes accessed | tf_op | source)
XLA Modules:
  0.0 614.1 jit_solution(6813895752519994719)
XLA Ops:
  6.5 2.4 stack.2
  8.9 10.2 %all-to-all-start = ((bf16[8,8,7,16,128]{4,3,2,1,0:T(8,128)(2,1)}), bf16[8,8,7,16,128]{4,3,2,1,0:T(8,128)(2,1)}, u32[]{:S(2)}, u32[]{:S(2)}) async-start(bf16[8,8,7,16,128]{4,3,2,1,0:T(8,128)(2,1)} %stack.2), calls=%async_computation | async-start | bytes 3670016 | tf_op jit(solution)/shard_map/all_to_all | solution.py:37
  19.2 1.9 collective-permute-start
  21.1 7.7 %collective-permute-start.1 = (bf16[256,128]{1,0:T(8,128)(2,1)S(1)}, bf16[256,128]{1,0:T(8,128)(2,1)S(1)}, u32[]{:S(2)}, u32[]{:S(2)}) collective-permute-start(bf16[256,128]{1,0:T(8,128)(2,1)S(1)} %get-tuple-element.12), channel_id=1, source_target_pairs={{8,0},{16,8},{24,16},{32,24},{40,32},{48,40},{56,48},{64,56},{72,6... | collective-permute-start | bytes 196616 | tf_op jit(solution)/shard_map/ppermute | solution.py:19
  28.9 1.8 collective-permute-done.1
  30.7 2.1 gather_fusion
  32.8 5.3 all-to-all-done
  38.1 2.2 copy.8
  40.3 0.7 fusion.6
  40.9 11.3 %collective-permute-start.3 = (bf16[256,128]{1,0:T(8,128)(2,1)S(1)}, bf16[256,128]{1,0:T(8,128)(2,1)S(1)}, u32[]{:S(2)}, u32[]{:S(2)}) collective-permute-start(bf16[256,128]{1,0:T(8,128)(2,1)S(1)} %bitcast.90), channel_id=1, source_target_pairs={{8,0},{16,8},{24,16},{32,24},{40,32},{48,40},{56,48},{64,56},{72,6... | collective-permute-start | bytes 196616 | tf_op jit(solution)/shard_map/ppermute | solution.py:19
  52.2 1.9 collective-permute-start.2
  54.2 7.3 %collective-permute-done.2 = bf16[256,128]{1,0:T(8,128)(2,1)S(1)} collective-permute-done((bf16[256,128]{1,0:T(8,128)(2,1)S(1)}, bf16[256,128]{1,0:T(8,128)(2,1)S(1)}, u32[]{:S(2)}, u32[]{:S(2)}) %collective-permute-start.2) | collective-permute-done | bytes 65568 | tf_op jit(solution)/shard_map/ppermute | solution.py:16
  61.4 2.1 gather_fusion.1
  63.5 2.1 fusion.3
  65.7 1.9 collective-permute-start.4
  67.7 7.3 %collective-permute-start.5 = (bf16[256,128]{1,0:T(8,128)(2,1)S(1)}, bf16[256,128]{1,0:T(8,128)(2,1)S(1)}, u32[]{:S(2)}, u32[]{:S(2)}) collective-permute-start(bf16[256,128]{1,0:T(8,128)(2,1)S(1)} %get-tuple-element.8), channel_id=1, source_target_pairs={{8,0},{16,8},{24,16},{32,24},{40,32},{48,40},{56,48},{64,56},{72,6... | collective-permute-start | bytes 196616 | tf_op jit(solution)/shard_map/ppermute | solution.py:19
  74.9 1.9 collective-permute-done.5
  76.8 2.1 gather_fusion.2
  78.9 2.1 fusion.4
  81.1 1.9 collective-permute-start.6
  83.1 7.3 %collective-permute-start.7 = (bf16[256,128]{1,0:T(8,128)(2,1)S(1)}, bf16[256,128]{1,0:T(8,128)(2,1)S(1)}, u32[]{:S(2)}, u32[]{:S(2)}) collective-permute-start(bf16[256,128]{1,0:T(8,128)(2,1)S(1)} %get-tuple-element.6), channel_id=1, source_target_pairs={{8,0},{16,8},{24,16},{32,24},{40,32},{48,40},{56,48},{64,56},{72,6... | collective-permute-start | bytes 196616 | tf_op jit(solution)/shard_map/ppermute | solution.py:19
  90.4 0.8 fusion.11
  91.2 5.8 all-to-all-start.2
  97.0 2.1 gather_fusion.3
  99.1 3.0 fusion.8
  102.1 1.1 all-to-all-done.2
  103.1 4.7 all-to-all-start.1
  107.8 0.2 copy.11
  108.0 5.9 all-to-all-done.1
  113.9 2.7 fusion.17
  116.8 487.1 %all-reduce.2.cloned.1.call-done = f32[1024,1024]{1,0:T(8,128)} async-done(((f32[1024,1024]{1,0:T(8,128)}), f32[1024,1024]{1,0:T(8,128)}) %all-reduce.2.cloned.1.call-update) | async-done | bytes 4194320 | tf_op jit(solution)/shard_map/psum | solution.py:57
  603.9 3.4 fusion.7
  (27 shorter events, 0.6 us)
Async XLA Ops:
  8.9 10.2 %copy-start.1 = (bf16[1024,128]{1,0:T(8,128)(2,1)S(1)}, bf16[1024,128]{1,0:T(8,128)(2,1)}, u32[]{:S(2)}) copy-start(bf16[1024,128]{1,0:T(8,128)(2,1)} %param.5) | copy-start | bytes 786436
  8.9 19.9 %copy-start.2 = (s32[8,7]{1,0:T(8,128)S(1)}, s32[8,7]{1,0:T(8,128)}, u32[]{:S(2)}) copy-start(s32[8,7]{1,0:T(8,128)} %param.4) | copy-start | bytes 676
  8.9 29.1 %all-to-all-start = ((bf16[8,8,7,16,128]{4,3,2,1,0:T(8,128)(2,1)}), bf16[8,8,7,16,128]{4,3,2,1,0:T(8,128)(2,1)}, u32[]{:S(2)}, u32[]{:S(2)}) async-start(bf16[8,8,7,16,128]{4,3,2,1,0:T(8,128)(2,1)} %stack.2), calls=%async_computation | async-start | bytes 3670016 | tf_op jit(solution)/shard_map/all_to_all | solution.py:37
  19.2 9.8 %collective-permute-start = (bf16[256,128]{1,0:T(8,128)(2,1)S(1)}, bf16[256,128]{1,0:T(8,128)(2,1)S(1)}, u32[]{:S(2)}, u32[]{:S(2)}) collective-permute-start(bf16[256,128]{1,0:T(8,128)(2,1)S(1)} %get-tuple-element.11), channel_id=1, source_target_pairs={{0,8},{8,16},{16,24},{24,32},{32,40},{40,48},{48,56},{56,64},{64,7... | collective-permute-start | bytes 196616 | tf_op jit(solution)/shard_map/ppermute | solution.py:16
  21.1 9.6 %collective-permute-start.1 = (bf16[256,128]{1,0:T(8,128)(2,1)S(1)}, bf16[256,128]{1,0:T(8,128)(2,1)S(1)}, u32[]{:S(2)}, u32[]{:S(2)}) collective-permute-start(bf16[256,128]{1,0:T(8,128)(2,1)S(1)} %get-tuple-element.12), channel_id=1, source_target_pairs={{8,0},{16,8},{24,16},{32,24},{40,32},{48,40},{56,48},{64,56},{72,6... | collective-permute-start | bytes 196616 | tf_op jit(solution)/shard_map/ppermute | solution.py:19
  38.1 2.2 copy-start
  40.9 13.2 %collective-permute-start.3 = (bf16[256,128]{1,0:T(8,128)(2,1)S(1)}, bf16[256,128]{1,0:T(8,128)(2,1)S(1)}, u32[]{:S(2)}, u32[]{:S(2)}) collective-permute-start(bf16[256,128]{1,0:T(8,128)(2,1)S(1)} %bitcast.90), channel_id=1, source_target_pairs={{8,0},{16,8},{24,16},{32,24},{40,32},{48,40},{56,48},{64,56},{72,6... | collective-permute-start | bytes 196616 | tf_op jit(solution)/shard_map/ppermute | solution.py:19
  52.2 9.2 %collective-permute-start.2 = (bf16[256,128]{1,0:T(8,128)(2,1)S(1)}, bf16[256,128]{1,0:T(8,128)(2,1)S(1)}, u32[]{:S(2)}, u32[]{:S(2)}) collective-permute-start(bf16[256,128]{1,0:T(8,128)(2,1)S(1)} %bitcast.89), channel_id=1, source_target_pairs={{0,8},{8,16},{16,24},{24,32},{32,40},{40,48},{48,56},{56,64},{64,7... | collective-permute-start | bytes 196616 | tf_op jit(solution)/shard_map/ppermute | solution.py:16
  65.7 9.2 %collective-permute-start.4 = (bf16[256,128]{1,0:T(8,128)(2,1)S(1)}, bf16[256,128]{1,0:T(8,128)(2,1)S(1)}, u32[]{:S(2)}, u32[]{:S(2)}) collective-permute-start(bf16[256,128]{1,0:T(8,128)(2,1)S(1)} %get-tuple-element.7), channel_id=1, source_target_pairs={{0,8},{8,16},{16,24},{24,32},{32,40},{40,48},{48,56},{56,64},{64,7... | collective-permute-start | bytes 196616 | tf_op jit(solution)/shard_map/ppermute | solution.py:16
  67.7 9.1 %collective-permute-start.5 = (bf16[256,128]{1,0:T(8,128)(2,1)S(1)}, bf16[256,128]{1,0:T(8,128)(2,1)S(1)}, u32[]{:S(2)}, u32[]{:S(2)}) collective-permute-start(bf16[256,128]{1,0:T(8,128)(2,1)S(1)} %get-tuple-element.8), channel_id=1, source_target_pairs={{8,0},{16,8},{24,16},{32,24},{40,32},{48,40},{56,48},{64,56},{72,6... | collective-permute-start | bytes 196616 | tf_op jit(solution)/shard_map/ppermute | solution.py:19
  81.1 15.9 %collective-permute-start.6 = (bf16[256,128]{1,0:T(8,128)(2,1)S(1)}, bf16[256,128]{1,0:T(8,128)(2,1)S(1)}, u32[]{:S(2)}, u32[]{:S(2)}) collective-permute-start(bf16[256,128]{1,0:T(8,128)(2,1)S(1)} %get-tuple-element.5), channel_id=1, source_target_pairs={{0,8},{8,16},{16,24},{24,32},{32,40},{40,48},{48,56},{56,64},{64,7... | collective-permute-start | bytes 196616 | tf_op jit(solution)/shard_map/ppermute | solution.py:16
  83.1 13.9 %collective-permute-start.7 = (bf16[256,128]{1,0:T(8,128)(2,1)S(1)}, bf16[256,128]{1,0:T(8,128)(2,1)S(1)}, u32[]{:S(2)}, u32[]{:S(2)}) collective-permute-start(bf16[256,128]{1,0:T(8,128)(2,1)S(1)} %get-tuple-element.6), channel_id=1, source_target_pairs={{8,0},{16,8},{24,16},{32,24},{40,32},{48,40},{56,48},{64,56},{72,6... | collective-permute-start | bytes 196616 | tf_op jit(solution)/shard_map/ppermute | solution.py:19
  91.2 12.0 %all-to-all-start.2 = ((bf16[8,128,128]{2,1,0:T(8,128)(2,1)}), bf16[8,128,128]{2,1,0:T(8,128)(2,1)S(1)}, u32[]{:S(2)}, u32[]{:S(2)}) async-start(bf16[8,128,128]{2,1,0:T(8,128)(2,1)} %fusion.11), calls=%async_computation.2 | async-start | bytes 524288 | tf_op jit(solution)/shard_map/all_to_all | solution.py:51
  103.1 10.8 %all-to-all-start.1 = ((bf16[8,128,128]{1,2,0:T(8,128)(2,1)}), bf16[8,128,128]{1,2,0:T(8,128)(2,1)S(1)}, u32[]{:S(2)}, u32[]{:S(2)}) async-start(bf16[8,128,128]{1,2,0:T(8,128)(2,1)} %fusion.8), calls=%async_computation.1 | async-start | bytes 524288 | tf_op jit(solution)/shard_map/all_to_all | solution.py:52
  107.8 496.0 %all-reduce.2.cloned.1.call-start = ((), (), s32[]{:S(2)}) async-start(), calls=%async_computation.3 | async-start | bytes 8388608 | tf_op jit(solution)/shard_map/psum | solution.py:57
Sparse Core Ops, SparseCore 0:
  116.8 487.0 all-reduce.1
